TPU v7x, 256 devices: a whole 4x4x8 slice. The times are simulated.
256 devices in a mesh: seq: 64 (over y, z, core), section: 4 (over x).
Axes of the slice: x: 4, y: 4, z: 8, core: 2. Of those that a mesh axis runs over, the one named last changes fastest.
Arguments:
- acts: bfloat16 [16384, 1408], P('seq'), may hold values from -16 to 16
- pre_act: bfloat16 [16384, 1536], P('seq', 'section'), may hold values from -6 to 6
- emb_grad: bfloat16 [8192, 1536], P('seq', 'section'), may hold values from -6 to 6
- filters: bfloat16 [7040, 1536], P('seq', 'section'), may hold values from -0.0625 to 0.0625
Outputs:
- input_grad: bfloat16 [16384, 1408], P('seq', 'section')
- filter_grad: float32 [7040, 1536], P('seq', 'section')
All inputs are finite; a program needn't handle non-finite values.
Results may differ from a plain program's by a relative error of at most 0.0049.
Values may be sent and summed in bfloat16 or wider, within the bound.
A program may use at most 128 MiB of HBM per device.

v0:
```python
import math

import jax
import jax.numpy as jnp
from jax import lax
from jax.sharding import PartitionSpec as P

KERNEL = 5
SEQS = 1


def with_halo(shard, sides, width):
    for axis, dim in sides:
        size, length = (lax.axis_size(axis), shard.shape[dim])
        up = [(i, (i + 1) % size) for i in range(size - 1)]
        down = [(j, i) for i, j in up]
        last = lax.slice_in_dim(shard, length - width, length, axis=dim)
        first = lax.slice_in_dim(shard, 0, width, axis=dim)
        before = lax.ppermute(last, axis, up)
        after = lax.ppermute(first, axis, down)
        shard = jnp.concatenate([before, shard, after], axis=dim)
    return shard


def gelu_slope(value):
    cumul = 0.5 * (1.0 + lax.erf(value * 0.7071067811865476))
    dens = jnp.exp(-0.5 * value * value) * 0.3989422804014327
    return cumul + value * dens


def shards(acts, pre_act, emb_grad, filters):
    rows = acts.shape[0]
    c_in = acts.shape[1]
    upward = jnp.repeat(emb_grad.astype(jnp.float32), 2, axis=0) * 0.5
    zvalue = pre_act.astype(jnp.float32)
    dz_grad = (upward * gelu_slope(zvalue)).astype(jnp.bfloat16)
    total_rows = rows * lax.axis_size("seq")
    length = total_rows // SEQS
    first = lax.axis_index("seq") * rows
    positions = first - 2 + jnp.arange(rows + 4, dtype=jnp.int32)
    inside = (jnp.floor_divide(positions, length) == first // length).astype(jnp.bfloat16)[:, None]
    scale_value = 1.0 / math.sqrt(total_rows)
    grad_rim = with_halo(dz_grad, (("seq", 0),), 2) * inside
    whole_term = (
        jnp.concatenate(
            [
                jnp.einsum(
                    "rc,ro->co",
                    acts,
                    grad_rim[4 - k : 4 - k + rows],
                    preferred_element_type=jnp.float32,
                )
                for k in range(KERNEL)
            ],
            axis=0,
        )
        * scale_value
    )
    piece = lax.all_gather(filters, "seq", axis=0, tiled=True)
    width = piece.shape[0]
    product = jnp.einsum("ro,no->rn", grad_rim, piece, preferred_element_type=jnp.float32)
    tap_of = jnp.arange(width, dtype=jnp.int32) // c_in
    total = jnp.zeros((rows, width), jnp.float32)
    for k in range(KERNEL):
        total = total + jnp.where((tap_of == k)[None, :], product[4 - k : 4 - k + rows], 0.0)
    partial_input = total.reshape(rows, KERNEL, c_in).sum(axis=1)
    input_grad = lax.psum_scatter(partial_input, "section", scatter_dimension=1, tiled=True).astype(
        jnp.bfloat16
    )
    filter_grad = lax.psum_scatter(whole_term, "seq", scatter_dimension=0, tiled=True)
    return (input_grad, filter_grad)


def solution(mesh):
    in_specs = (P("seq", None), P("seq", "section"), P("seq", "section"), P("seq", "section"))
    out_specs = (P("seq", "section"), P("seq", "section"))
    return jax.shard_map(shards, mesh=mesh, in_specs=in_specs, out_specs=out_specs, check_vma=False)
```

profile of v0, /device:TPU:6, one launch (start us, length us, event | category | flops | bytes accessed | tf_op | source)
XLA Modules:
  0.0 340.7 jit_solution(12863627836406627910)
XLA Ops:
  7.2 0.0 all-gather.3.cloned.1.call-start
  7.2 0.7 all-gather.3.cloned.1.call-update
  7.9 0.0 all-reduce.3.cloned.1.call-start
  8.0 0.9 convert_multiply_fusion.4
  8.9 0.1 broadcast_in_dim.46
  9.0 0.3 mul.55
  9.3 1.1 fusion.16
  10.4 1.3 collective-permute-start.1
  11.7 3.0 collective-permute-start
  14.8 0.8 collective-permute-done
  15.6 0.1 maximum_multiply_fusion
  15.7 0.5 fusion.8
  16.2 0.5 fusion.7
  16.7 0.5 fusion.6
  17.2 0.5 fusion.5
  17.7 0.5 fusion.4
  18.2 4.6 %broadcast_multiply_fusion = f32[7040,384]{0,1:T(8,128)} fusion(f32[7040,384]{0,1:T(8,128)S(1)} %fusion.4), kind=kLoop, calls=%fused_computation.9 | loop fusion | flops 2703360 | bytes 21626880 | tf_op jit(solution)/shard_map/mul | solution.py:45
  22.8 0.0 all-reduce.3.cloned.1.call-update
  22.9 0.0 reduce-scatter.3.cloned.1.call-start
  23.0 70.9 %all-gather.3.cloned.1.call-done = bf16[64,110,384]{2,1,0:T(8,128)(2,1)} async-done(((bf16[1,110,384]{2,1,0:T(8,128)(2,1)}), bf16[64,110,384]{2,1,0:T(8,128)(2,1)}) %all-gather.3.cloned.1.call-update) | async-done | bytes 5406736 | tf_op jit(solution)/shard_map/all_gather | solution.py:59
  93.9 7.7 %reshape.59 = bf16[7040,384]{1,0:T(8,128)(2,1)} reshape(bf16[64,110,384]{2,1,0:T(8,128)(2,1)} %all-gather.3.cloned.1.call-done) | data formatting | bytes 10813440
  101.6 4.7 %fusion.30 = f32[260,7040]{1,0:T(8,128)S(1)} fusion(bf16[7040,384]{1,0:T(8,128)(2,1)} %reshape.59, bf16[2,384]{1,0:T(2,128)(2,1)S(1)} %collective-permute-done.1, bf16[256,384]{1,0:T(8,128)(2,1)S(1)} %fusion.16, bf16[2,384]{1,0:T(2,128)(2,1)S(1)} %collective-permute-done, bf16[260]{0:T(512)(128)(2,1)S(1)} %fusion.29), kind=kOutput, calls=%fused_computation.63 | convolution fusion | flops 1406545920 | bytes 12928520 | tf_op jit(solution)/shard_map/ro,no->rn/dot_general | solution.py:61
  106.3 6.0 %fusion = f32[256,7040]{1,0:T(8,128)} fusion(f32[260,7040]{1,0:T(8,128)S(1)} %fusion.30, pred[7040]{0:T(1024)(128)(4,1)S(1)} %get-tuple-element.10, pred[7040]{0:T(1024)(128)(4,1)S(1)} %get-tuple-element.11, pred[7040]{0:T(1024)(128)(4,1)S(1)} %get-tuple-element.12, pred[7040]{0:T(1024)(128)(4,1)S(1)} %broadcast_compare_fusion.4, ...), kind=kLoop, calls=%fused_computation.1 | loop fusion | flops 16220160 | bytes 43288960 | tf_op jit(solution)/shard_map/add | solution.py:65
  112.3 8.7 %copy.9 = f32[256,7040]{0,1:T(8,128)} copy(f32[256,7040]{1,0:T(8,128)} %fusion) | data formatting | bytes 14417920 | tf_op jit(solution)/shard_map/add | solution.py:65
  121.1 5.0 %reduce_sum.9 = f32[256,1408]{0,1:T(8,128)} reduce(f32[256,5,1408]{0,2,1:T(8,128)} %bitcast.31, f32[]{:T(128)} %constant.61.clone.1), dimensions={1}, to_apply=%region_0.1 | reduce | flops 1441792 | bytes 8650756 | tf_op jit(solution)/shard_map/reduce_sum | solution.py:66
  126.1 0.0 reduce-scatter.3.cloned.1.call-update
  126.1 0.6 dynamic-slice
  127.3 177.9 %all-reduce.3.cloned.1.call-done = f32[7040,384]{0,1:T(8,128)} async-done(((f32[7040,384]{0,1:T(8,128)}), f32[7040,384]{0,1:T(8,128)}) %all-reduce.3.cloned.1.call-update) | async-done | bytes 10813456
  305.2 1.1 constant_dynamic-slice_fusion
  306.3 0.8 copy.10
  307.2 25.3 %reduce-scatter.3.cloned.1.call-done = f32[256,352]{0,1:T(8,128)} async-done(((f32[256,1408]{0,1:T(8,128)}), f32[256,352]{0,1:T(8,128)}) %reduce-scatter.3.cloned.1.call-update) | async-done | bytes 360464 | tf_op jit(solution)/shard_map/reduce_scatter | solution.py:67
  332.5 1.7 convert_element_type.23
  (12 shorter events, 0.1 us)
Async XLA Ops:
  7.2 8.5 %copy-start = (bf16[256,1408]{1,0:T(8,128)(2,1)S(1)}, bf16[256,1408]{1,0:T(8,128)(2,1)}, u32[]{:S(2)}) copy-start(bf16[256,1408]{1,0:T(8,128)(2,1)} %param.4) | copy-start | bytes 2162692
  7.2 86.7 %all-gather.3.cloned.1.call-start = ((), (), s32[]{:S(2)}) async-start(), calls=%async_computation.2 | async-start | bytes 5591040 | tf_op jit(solution)/shard_map/all_gather | solution.py:59
  7.9 297.3 %all-reduce.3.cloned.1.call-start = ((), (), s32[]{:S(2)}) async-start(), calls=%async_computation.3 | async-start | bytes 21626880
  10.4 4.4 %collective-permute-start.1 = (bf16[2,384]{1,0:T(2,128)(2,1)S(1)}, bf16[2,384]{1,0:T(2,128)(2,1)S(1)}, u32[]{:S(2)}, u32[]{:S(2)}) collective-permute-start(bf16[2,384]{1,0:T(2,128)(2,1)S(1)} %get-tuple-element.9), channel_id=1, source_target_pairs={{4,0},{8,4},{12,8},{16,12},{20,16},{24,20},{28,24},{32,28},{36,32}... | collective-permute-start | bytes 4616 | tf_op jit(solution)/shard_map/ppermute | solution.py:20
  11.7 3.8 %collective-permute-start = (bf16[2,384]{1,0:T(2,128)(2,1)S(1)}, bf16[2,384]{1,0:T(2,128)(2,1)S(1)}, u32[]{:S(2)}, u32[]{:S(2)}) collective-permute-start(bf16[2,384]{1,0:T(2,128)(2,1)S(1)} %get-tuple-element.8), channel_id=1, source_target_pairs={{0,4},{4,8},{8,12},{12,16},{16,20},{20,24},{24,28},{28,32},{32,36}... | collective-permute-start | bytes 4616 | tf_op jit(solution)/shard_map/ppermute | solution.py:19
  22.9 309.6 %reduce-scatter.3.cloned.1.call-start = ((), (), s32[]{:S(2)}) async-start(), calls=%async_computation.1 | async-start | bytes 1802240 | tf_op jit(solution)/shard_map/reduce_scatter | solution.py:67
  112.3 221.8 %copy-start.1 = (bf16[256,1408]{1,0:T(8,128)(2,1)S(1)}, bf16[256,1408]{1,0:T(8,128)(2,1)}, u32[]{:S(2)}) copy-start(bf16[256,1408]{1,0:T(8,128)(2,1)} %param.4) | copy-start | bytes 2162692
  121.1 5.0 %copy-start.2 = (u32[256]{0:T(256)S(1)}, u32[256]{0:T(256)}, u32[]{:S(2)}) copy-start(u32[256]{0:T(256)} %constant.69) | copy-start | bytes 3076
Sparse Core Ops, SparseCore 0:
  10.7 83.1 all-gather.2
  97.5 207.6 all-reduce.2
  308.0 24.4 reduce-scatter.2
where the time goes:
time: 343 us; the launch traced here: 341 us
  waiting for transfers between devices  276 us (80%)
  other arithmetic  19.5 us (6%)
  local copies, waits for them, and re-layouts  19.4 us (6%)
  between operations  14.6 us (4%)
  matrix products  7.19 us (2%)
  starting transfers between devices  4.44 us (1%)
    unnamed x4, waiting for transfers between devices  179 us
    all_gather x1, waiting for transfers between devices, shards(): piece = lax.all_gather(filters, 'seq', axis=0, tiled=True)  70.9 us
    reduce_scatter x1, waiting for transfers between devices, shards(): lax.psum_scatter(partial_input, 'section', scatter_dimension=1, tiled=True)  25.3 us
    unnamed x10, local copies, waits for them, and re-layouts  10.3 us
    add x1, local copies, waits for them, and re-layouts, shards(): total + jnp.where((tap_of == k)[None, :], product[4 - k:4 - k + rows], 0.0)  8.73 us
  transfers between devices with their start and end apart: 5, of which 4 were waited for; matrix products, arithmetic and copies ran while one was open for 13% of the time, Pallas kernels for 0%

commit v1 on v0

v1 whole, which is shorter than its diff:
```python
import functools
import math

import jax
import jax.numpy as jnp
from jax import lax
from jax.experimental import pallas as pl
from jax.experimental.pallas import tpu as pltpu
from jax.sharding import PartitionSpec as P

MESH = pl.DeviceIdType.MESH
F32, BF16 = jnp.float32, jnp.bfloat16
TAPS = 5
NY, NZ, NX = 4, 8, 4
SHARDS = 64
C_IN = 1408
ROWS = 256
PART = 384
OWN = 110
PAD = 112
SLOT = 128
SLICE = C_IN // NX
SPAN = C_IN + 256


def gelu_slope(value):
    cumul = 0.5 * (1.0 + lax.erf(value * 0.7071067811865476))
    dens = jnp.exp(-0.5 * value * value) * 0.3989422804014327
    return cumul + value * dens


def nt_dot(a, b):
    return lax.dot_general(a, b, (((1,), (1,)), ((), ())), preferred_element_type=F32)


def wrap(value, size):
    return lax.rem(value + 2 * size, size)


def kernel(scale, acts, pre, emb, filt, ig_out, fg_out, slots, packed, window, rim, dz, part, send_r, send_l, recv_r, recv_l,
           small_sr, small_sl, small_rr, small_rl, halo_s, halo_r, ig_own, ig_s, ig_r, sems, gather_sem, sib_sem, red_sem, x_sem):
    s = lax.axis_index("seq")
    x = lax.axis_index("section")
    y, z, h = s // 16, lax.rem(s, 16) // 2, lax.rem(s, 2)

    def at(yy, zz, hh):
        return (wrap(yy, NY) * 16 + wrap(zz, NZ) * 2 + hh, x)

    sibling = (s + 1 - 2 * h, x)
    after = (lax.rem(s + 1, SHARDS), x)
    before = (lax.rem(s + SHARDS - 1, SHARDS), x)
    pending = []

    def send(src, dst, ssem, rsem, to):
        copy = pltpu.make_async_remote_copy(src_ref=src, dst_ref=dst, send_sem=ssem, recv_sem=rsem, device_id=to, device_id_type=MESH)
        copy.start()
        return copy

    def arrive(dst, rsem):
        pltpu.make_async_remote_copy(src_ref=dst, dst_ref=dst, send_sem=rsem, recv_sem=rsem, device_id=sibling, device_id_type=MESH).wait_recv()

    here = pl.ds(pl.multiple_of(h * ROWS, ROWS), ROWS)
    load_acts = pltpu.make_async_copy(acts, window.at[here, pl.ds(0, C_IN)], sems.at[0])
    load_acts.start()

    block = jnp.concatenate([filt[...].astype(F32), jnp.zeros((SLOT - OWN, PART), F32)], axis=0)
    shift = lax.rem(s * OWN, 16)
    slots[h, y, z] = pltpu.roll(block, shift, 0).astype(BF16)

    barrier = pltpu.get_barrier_semaphore()
    cross = (jnp.where(h == 0, before[0], after[0]), x)
    peers = [at(y + 1, z, h), at(y - 1, z, h), at(y, z + 1, h), at(y, z - 1, h), sibling, cross]
    peers += [(s, lax.rem(x + i, NX)) for i in range(1, NX)]
    for peer in peers:
        pl.semaphore_signal(barrier, inc=1, device_id=peer, device_id_type=MESH)
    pl.semaphore_wait(barrier, len(peers))

    def make_dz():
        pick = (lax.broadcasted_iota(jnp.int32, (ROWS, ROWS // 2), 0) // 2
                == lax.broadcasted_iota(jnp.int32, (ROWS, ROWS // 2), 1)).astype(BF16)
        up = jnp.dot(pick, emb[...], preferred_element_type=F32) * 0.5
        rim[8:8 + ROWS, :] = (up * gelu_slope(pre[...].astype(F32))).astype(BF16).astype(F32)
        halo_s[0] = rim[8:24, :].astype(BF16)
        halo_s[1] = rim[8 + ROWS - 16:8 + ROWS, :].astype(BF16)

    def send_halo():
        pending.append(send(halo_s.at[0], halo_r.at[0], sems.at[1], sems.at[3], before))
        pending.append(send(halo_s.at[1], halo_r.at[1], sems.at[2], sems.at[4], after))

    def make_taps():
        arrive(halo_r.at[0], sems.at[3])
        arrive(halo_r.at[1], sems.at[4])
        low = jnp.where(s > 0, 1.0, 0.0)
        high = jnp.where(s < SHARDS - 1, 1.0, 0.0)
        rim[0:8, :] = halo_r[1].astype(F32)[8:16] * low
        rim[8 + ROWS:16 + ROWS, :] = halo_r[0].astype(F32)[0:8] * high
        for k in range(TAPS):
            dz[k, here, :] = rim[10 - k:10 - k + ROWS, :].astype(BF16)
        pending.append(send(dz.at[:, here], dz.at[:, here], sems.at[5], sems.at[6], sibling))

    def send_acts():
        load_acts.wait()
        lanes = window.at[here, pl.ds(0, C_IN)]
        pending.append(send(lanes, lanes, sems.at[7], sems.at[8], sibling))

    def sibling_inputs():
        there = pl.ds(pl.multiple_of((1 - h) * ROWS, ROWS), ROWS)
        arrive(window.at[there, pl.ds(0, C_IN)], sems.at[8])
        arrive(dz.at[:, there], sems.at[6])
        window[:, C_IN:SPAN] = window[:, 0:SPAN - C_IN]

    def partial(yy, zz):
        owner = yy * 16 + zz * 2 + h
        start = owner * OWN
        tap = start // C_IN
        column = start - tap * C_IN
        tile = column // 128
        off = column - tile * 128
        rest = C_IN - column
        row = lax.broadcasted_iota(jnp.int32, (PAD, 256), 0)
        lane = lax.broadcasted_iota(jnp.int32, (PAD, 256), 1)
        seen = window[:, pl.ds(pl.multiple_of(tile * 128, 128), 256)]
        hit = (lane - row == off) & (row < jnp.minimum(OWN, rest))
        chosen = nt_dot(jnp.where(hit, 1.0, 0.0).astype(BF16), seen).astype(BF16)
        part[yy, zz] = jnp.dot(chosen, dz[tap], preferred_element_type=F32)

        @pl.when(rest < OWN)
        def _():
            hit2 = (lane - row == off) & (row >= rest) & (row < OWN)
            chosen2 = nt_dot(jnp.where(hit2, 1.0, 0.0).astype(BF16), seen).astype(BF16)
            part[yy, zz] += jnp.dot(chosen2, dz[lax.rem(tap + 1, TAPS)], preferred_element_type=F32)

    def pack():
        packed[0:16, :] = jnp.zeros((16, PART), BF16)

        def one(i, carry):
            for j in range(8):
                base = pl.multiple_of(i * (8 * OWN) + (j * OWN) // 16 * 16, 16)
                block = slots[j % 2, i // 2, lax.rem(i, 2) * 4 + j // 2]
                packed[pl.ds(base, 16), :] += block[0:16]
                packed[pl.ds(base + 16, SLOT - 16), :] = block[16:SLOT]
            return carry

        lax.fori_loop(0, SHARDS // 8, one, 0)

    def input_grad():
        def one(i, carry):
            dest = lax.rem(x + 1 + i, NX)
            total = jnp.zeros((SLICE, ROWS), F32)
            for k in range(TAPS):
                rows = packed[pl.ds(pl.multiple_of(k * C_IN + dest * SLICE, 16), SLICE), :]
                total += nt_dot(rows, dz[k, here, :])

            @pl.when(i < NX - 1)
            def _():
                ig_s[i] = total.astype(BF16)
                send(ig_s.at[i], ig_r.at[i], x_sem.at[0, i], x_sem.at[1, i], (s, dest))

            @pl.when(i == NX - 1)
            def _():
                ig_own[...] = total

            return carry

        lax.fori_loop(0, NX, one, 0)

    def finish_input_grad():
        total = ig_own[...]
        for i in range(NX - 1):
            arrive(ig_r.at[i], x_sem.at[1, i])
            total += ig_r[i].astype(F32)
        ig_out[...] = total.T.astype(BF16)
        for i in range(NX - 1):
            pltpu.make_async_remote_copy(src_ref=ig_s.at[i], dst_ref=ig_r.at[i], send_sem=x_sem.at[0, i], recv_sem=x_sem.at[1, i],
                                         device_id=sibling, device_id_type=MESH).wait_send()

    def ring(axis, step):
        return at(y + step, z, h) if axis == "y" else at(y, z + step, h)

    def run(hh, done):
        first, second = ("z", "y") if hh == 0 else ("y", "z")
        n1, n2 = (NZ, NY) if hh == 0 else (NY, NZ)
        p1, p2 = (z, y) if hh == 0 else (y, z)
        counts = {"g": 0, "sib": 0}
        waits = []

        def slab(a, b, lo=None, size=None):
            a = pl.ds(lo, size) if a is None else a
            return slots.at[hh, b, a] if hh == 0 else slots.at[hh, a, b]

        def push(ref, axis, step, sem):
            done.append(send(ref, ref, gather_sem.at[0, sem], gather_sem.at[1, sem], ring(axis, step)))

        def share(ref):
            i = counts["sib"]
            counts["sib"] += 1
            done.append(send(ref, ref, sib_sem.at[0, i], sib_sem.at[1, i], sibling))

        def g_first(t):
            if t == 0:
                ref = slab(p1, p2)
                push(ref, first, 1, 0)
                push(ref, first, -1, 4)
                share(ref)
                return
            ref = slab(wrap(p1 - t, n1), p2)
            arrive(ref, gather_sem.at[1, t - 1])
            if t < n1 // 2:
                push(ref, first, 1, t)
            share(ref)
            if t < n1 // 2:
                ref = slab(wrap(p1 + t, n1), p2)
                arrive(ref, gather_sem.at[1, 4 + t - 1])
                if t < n1 // 2 - 1:
                    push(ref, first, -1, 4 + t)
                share(ref)

        half = n1 // 2

        def g_second(t):
            if t == 0:
                ref = slab(None, p2, 0, n1)
                push(ref, second, 1, 8)
                push(ref, second, -1, 12)
                return
            last = t == n2 // 2
            right, left = wrap(p2 - t, n2), wrap(p2 + t, n2)
            a = slab(None, right, 0, half if last else n1)
            arrive(a, gather_sem.at[1, 8 + t - 1])
            if t == n2 // 2 - 1:
                push(slab(None, right, 0, half), second, 1, 8 + t)
            elif not last:
                push(a, second, 1, 8 + t)
            b = slab(None, left, half if last else 0, half if last else n1)
            arrive(b, gather_sem.at[1, 12 + t - 1])
            if t == n2 // 2 - 1:
                push(slab(None, left, half, half), second, -1, 12 + t)
            elif not last:
                push(b, second, -1, 12 + t)
            share(a)
            share(b)

        def g_sibling():
            o = 1 - hh
            m1, m2 = (NZ, NY) if o == 0 else (NY, NZ)
            q1, q2 = (z, y) if o == 0 else (y, z)

            def other(a, b, lo=None, size=None):
                a = pl.ds(lo, size) if a is None else a
                return slots.at[o, b, a] if o == 0 else slots.at[o, a, b]

            i = 0
            for t in range(m1 // 2 + 1):
                arrive(other(wrap(q1 - t, m1), q2), sib_sem.at[1, i])
                i += 1
                if 0 < t < m1 // 2:
                    arrive(other(wrap(q1 + t, m1), q2), sib_sem.at[1, i])
                    i += 1
            mid = m1 // 2
            for t in range(1, m2 // 2 + 1):
                last = t == m2 // 2
                arrive(other(None, wrap(q2 - t, m2), 0, mid if last else m1), sib_sem.at[1, i])
                arrive(other(None, wrap(q2 + t, m2), mid if last else 0, mid if last else m1), sib_sem.at[1, i + 1])
                i += 2

        heavy, light = second, first
        nb = n1

        def cell(i, d):
            return (d, i) if hh == 0 else (i, d)

        def compute(d):
            d = wrap(d, n2)

            def body(i, carry):
                for j in range(2):
                    partial(*cell(2 * i + j, d))
                return carry

            lax.fori_loop(0, nb // 2, body, 0)

        def base(t):
            return 0 if t == 0 else half + (t - 1) * nb

        top = n2 // 2

        def r_heavy(t):
            for side in range(2):
                out, got, sign = (send_r, recv_r, 1) if side == 0 else (send_l, recv_l, -1)
                d = wrap(p2 + sign * (top - t), n2)
                lo, size = ((0 if side == 0 else half), half) if t == 0 else (0, nb)
                if t > 0:
                    plo, psize = ((0 if side == 0 else half), half) if t == 1 else (0, nb)
                    arrive(got.at[pl.ds(base(t - 1), psize)], red_sem.at[1, side * 4 + t - 1])
                for i in range(size):
                    value = part[cell(lo + i, d)]
                    if t > 0 and plo <= lo + i < plo + psize:
                        value = value + got[base(t - 1) + lo + i - plo].astype(F32)
                    out[base(t) + i] = value.astype(BF16)
                span = pl.ds(base(t), size)
                done.append(send(out.at[span], got.at[span], red_sem.at[0, side * 4 + t], red_sem.at[1, side * 4 + t], ring(heavy, sign)))

        def r_heavy_end():
            for side in range(2):
                got = recv_r if side == 0 else recv_l
                plo, psize = ((0 if side == 0 else half), half) if top == 1 else (0, nb)
                arrive(got.at[pl.ds(base(top - 1), psize)], red_sem.at[1, side * 4 + top - 1])
            for i in range(nb):
                part[cell(i, p2)] += recv_r[base(top - 1) + i].astype(F32) + recv_l[base(top - 1) + i].astype(F32)

        ltop = n1 // 2

        def r_light(t):
            for side in range(2):
                if side == 1 and t == 0:
                    continue
                out, got, sign = (small_sr, small_rr, 1) if side == 0 else (small_sl, small_rl, -1)
                d = wrap(p1 + sign * (ltop - t), n1)
                value = part[cell(d, p2)]
                if t > (0 if side == 0 else 1):
                    arrive(got.at[t - 1], red_sem.at[1, 8 + side * 4 + t - 1])
                    value = value + got[t - 1].astype(F32)
                out[t] = value.astype(BF16)
                done.append(send(out.at[t], got.at[t], red_sem.at[0, 8 + side * 4 + t], red_sem.at[1, 8 + side * 4 + t], ring(light, sign)))

        def r_end():
            t = ltop - 1
            arrive(small_rr.at[t], red_sem.at[1, 8 + t])
            arrive(small_rl.at[t], red_sem.at[1, 12 + t])
            total = part[cell(p1, p2)] + small_rr[t].astype(F32) + small_rl[t].astype(F32)
            fg_out[...] = total[0:OWN] * scale

        def whole_input_grad():
            g_sibling()
            pack()
            input_grad()

        g_first(0)
        send_acts()
        make_dz()
        send_halo()
        g_first(1)
        make_taps()
        g_first(2)
        if hh == 1:
            g_second(0)
            sibling_inputs()
            compute(p2 + 4)
            r_heavy(0)
            compute(p2 + 3)
            compute(p2 - 3)
            g_second(1)
            r_heavy(1)
            compute(p2 + 2)
            compute(p2 - 2)
            g_second(2)
            r_heavy(2)
            compute(p2 + 1)
            compute(p2 - 1)
            compute(p2)
            g_second(3)
            r_heavy(3)
            g_second(4)
            whole_input_grad()
            r_heavy_end()
            r_light(0)
            r_light(1)
            r_end()
        else:
            sibling_inputs()
            compute(p2 + 2)
            r_heavy(0)
            g_first(3)
            compute(p2 + 1)
            compute(p2 - 1)
            g_first(4)
            g_second(0)
            r_heavy(1)
            compute(p2)
            g_second(1)
            r_heavy_end()
            r_light(0)
            g_second(2)
            r_light(1)
            r_light(2)
            r_light(3)
            whole_input_grad()
            r_end()
        finish_input_grad()
        for copy in done:
            copy.wait_send()

    for hh in range(2):
        @pl.when(h == hh)
        def _(hh=hh):
            pending.clear()
            run(hh, pending)


def shards(acts, pre_act, emb_grad, filters):
    total_rows = acts.shape[0] * lax.axis_size("seq")
    vmem = pl.BlockSpec(memory_space=pltpu.VMEM)
    return pl.pallas_call(
        functools.partial(kernel, 1.0 / math.sqrt(total_rows)),
        out_shape=(jax.ShapeDtypeStruct((ROWS, SLICE), BF16), jax.ShapeDtypeStruct((OWN, PART), F32)),
        in_specs=[pl.BlockSpec(memory_space=pl.ANY), vmem, vmem, vmem],
        out_specs=(vmem, vmem),
        scratch_shapes=[
            pltpu.VMEM((2, NY, NZ, SLOT, PART), BF16),
            pltpu.VMEM((TAPS * C_IN + 16, PART), BF16),
            pltpu.VMEM((2 * ROWS, SPAN), BF16),
            pltpu.VMEM((ROWS + 16, PART), F32),
            pltpu.VMEM((TAPS, 2 * ROWS, PART), BF16),
            pltpu.VMEM((NY, NZ, PAD, PART), F32),
            pltpu.VMEM((14, PAD, PART), BF16),
            pltpu.VMEM((14, PAD, PART), BF16),
            pltpu.VMEM((14, PAD, PART), BF16),
            pltpu.VMEM((14, PAD, PART), BF16),
            pltpu.VMEM((4, PAD, PART), BF16),
            pltpu.VMEM((4, PAD, PART), BF16),
            pltpu.VMEM((4, PAD, PART), BF16),
            pltpu.VMEM((4, PAD, PART), BF16),
            pltpu.VMEM((2, 16, PART), BF16),
            pltpu.VMEM((2, 16, PART), BF16),
            pltpu.VMEM((SLICE, ROWS), F32),
            pltpu.VMEM((NX - 1, SLICE, ROWS), BF16),
            pltpu.VMEM((NX - 1, SLICE, ROWS), BF16),
            pltpu.SemaphoreType.DMA((9,)),
            pltpu.SemaphoreType.DMA((2, 16)),
            pltpu.SemaphoreType.DMA((2, 16)),
            pltpu.SemaphoreType.DMA((2, 16)),
            pltpu.SemaphoreType.DMA((2, NX - 1)),
        ],
        compiler_params=pltpu.CompilerParams(collective_id=0, has_side_effects=True, vmem_limit_bytes=56 << 20),
    )(acts, pre_act, emb_grad, filters)


def solution(mesh):
    in_specs = (P("seq", None), P("seq", "section"), P("seq", "section"), P("seq", "section"))
    out_specs = (P("seq", "section"), P("seq", "section"))
    return jax.shard_map(shards, mesh=mesh, in_specs=in_specs, out_specs=out_specs, check_vma=False)
```

time: 343 us -> 75.6 us (0.22)
  waiting for transfers between devices: 276 us -> 0 us
  Pallas kernels: 0 us -> 72.4 us
  other arithmetic: 19.5 us -> 0 us
  local copies, waits for them, and re-layouts: 19.4 us -> 2.44 us
  between operations: 14.6 us -> 0.65 us
  matrix products: 7.19 us -> 0 us
  starting transfers between devices: 4.44 us -> 0 us
    unnamed x4 -> x0, waiting for transfers between devices: 179 us -> none
    pallas_call x0 -> x1, Pallas kernels: none -> 72.4 us  [shards(): pl.pallas_call(functools.partial(kernel, 1.0 / math.sqrt(total_rows)), ou...]
    all_gather x1 -> x0, waiting for transfers between devices: 70.9 us -> none  [shards(): piece = lax.all_gather(filters, 'seq', axis=0, tiled=True)]
    reduce_scatter x1 -> x0, waiting for transfers between devices: 25.3 us -> none  [shards(): lax.psum_scatter(partial_input, 'section', scatter_dimension=1, tiled=True)]
    unnamed x10 -> x3, local copies, waits for them, and re-layouts: 10.3 us -> 0.67 us
    add x1 -> x0, local copies, waits for them, and re-layouts: 8.73 us -> none  [shards(): total + jnp.where((tap_of == k)[None, :], product[4 - k:4 - k + rows], 0.0)]
    dot_general x6 -> x0, matrix products: 7.19 us -> none  [the longest x1 4.7 us: shards(): jnp.einsum('ro,no->rn', grad_rim, piece, preferred_element_type=jnp.float32)]
    add x1 -> x0, other arithmetic: 5.99 us -> none  [shards(): total + jnp.where((tap_of == k)[None, :], product[4 - k:4 - k + rows], 0.0)]
  transfers between devices with their start and end apart: 5 -> 0, of which waited for: 4 -> 0; matrix products, arithmetic and copies ran while one was open for 13% -> 0% of each run, Pallas kernels for 0% -> 0%
where the time goes in v1:
time: 75.6 us; the launch traced here: 75.5 us
  Pallas kernels  72.4 us (96%)
  local copies, waits for them, and re-layouts  2.44 us (3%)
    pallas_call x1, Pallas kernels, shards(): pl.pallas_call(functools.partial(kernel, 1.0 / math.sqrt(total_rows)), ou...  72.4 us
    pallas_call x1, local copies, waits for them, and re-layouts, shards(): pl.pallas_call(functools.partial(kernel, 1.0 / math.sqrt(total_rows)), ou...  1.77 us

profile of v1, /device:TPU:6, one launch (start us, length us, event | category | flops | bytes accessed | tf_op | source)
XLA Modules:
  0.0 75.5 jit_solution(4024802463309222056)
XLA Ops:
  0.6 72.4 %shard_map.59 = (bf16[256,352]{1,0:T(8,128)(2,1)}, f32[110,384]{1,0:T(8,128)}) custom-call(bf16[256,1408]{1,0:T(8,128)(2,1)} %acts.1, bf16[256,384]{1,0:T(8,128)(2,1)} %pre.1, bf16[128,384]{1,0:T(8,128)(2,1)} %emb.1, bf16[110,384]{1,0:T(8,128)(2,1)} %filt.1), custom_call_target="tpu_custom_call" | custom-call | tf_op jit(solution)/shard_map/pallas_call | solution.py:403
  73.0 0.0 copy-start
  73.0 1.8 %copy.6 = bf16[256,352]{0,1:T(8,128)(2,1)} copy(bf16[256,352]{1,0:T(8,128)(2,1)} %get-tuple-element.2) | data formatting | bytes 360448 | tf_op jit(solution)/shard_map/pallas_call | solution.py:403
  74.8 0.0 copy-done
  74.8 0.7 copy.8
Async XLA Ops:
  73.0 1.8 %copy-start = (f32[110,384]{1,0:T(8,128)S(1)}, f32[110,384]{1,0:T(8,128)}, u32[]{:S(2)}) copy-start(f32[110,384]{1,0:T(8,128)} %get-tuple-element.7) | copy-start | bytes 506884

commit v2 on v0

v2 whole, which is shorter than its diff:
```python
import functools
import math

import jax
import jax.numpy as jnp
from jax import lax
from jax.experimental import pallas as pl
from jax.experimental.pallas import tpu as pltpu
from jax.sharding import PartitionSpec as P

MESH = pl.DeviceIdType.MESH
F32, BF16 = jnp.float32, jnp.bfloat16
I32 = jnp.int32
TAPS = 5
NX, NY, NZ = 4, 4, 8
GROUP = 8
SHARDS = 64
C_IN = 1408
ROWS = 256
PART = 384
OWN = 110
SLOT = 128
CHUNK = C_IN // GROUP
QUARTER = 48
SPACE = TAPS * CHUNK
SLICE = C_IN // NX
EDGE = 16


def gelu_slope(value):
    cumul = 0.5 * (1.0 + lax.erf(value * 0.7071067811865476))
    dens = jnp.exp(-0.5 * value * value) * 0.3989422804014327
    return cumul + value * dens


def nt_dot(a, b):
    return lax.dot_general(a, b, (((1,), (1,)), ((), ())), preferred_element_type=F32)


def iota(shape, axis):
    return lax.broadcasted_iota(I32, shape, axis)


def kernel(scale, acts, pre, emb, filt, ig_out, fg_out, f_out, f_in, f_slots, f_all, halo_p, halo_e, rim, dzx, dz, at_s, at, part,
           s_r, s_l, g_r, g_l, total_s, total_r, ig_own, ig_s, ig_r, fin_s, send_sem, recv_sem):
    s = lax.axis_index("seq")
    x = lax.axis_index("section")
    y, z, h = s // 16, lax.rem(s, 16) // 2, lax.rem(s, 2)
    j = 2 * y + h

    def at_place(yy, zz, hh):
        return lax.rem(yy + NY, NY) * 16 + lax.rem(zz + NZ, NZ) * 2 + hh

    def member(jj, zz):
        return (jj // 2) * 16 + zz * 2 + lax.rem(jj, 2)

    sibling = s + 1 - 2 * h
    after = lax.rem(s + 1, SHARDS)
    before = lax.rem(s + SHARDS - 1, SHARDS)

    def row_block(u):
        tile = (u * OWN) // 16 * 16
        chunk = (u * OWN) // CHUNK
        cut = (chunk + 1) * CHUNK - tile
        lead = u * OWN - tile
        return tile, chunk, cut, lead, cut < lead + OWN

    own_v, own_u = s // 8, lax.rem(s, 8)
    _, own_w, own_cut, own_lead, own_two = row_block(own_u)
    to_a = member(lax.rem(5 * own_v + own_w, GROUP), own_u)
    to_b = member(lax.rem(5 * own_v + own_w + 1, GROUP), own_u)
    my_tile, my_w, my_cut, my_lead, my_two = row_block(z)

    def tap_of(w):
        return lax.rem(2 * w + 3 * j, TAPS)

    def owner_of(w):
        return (8 * tap_of(w) + j) // 5 * 8 + z

    from_a, from_b = owner_of(my_w), owner_of(my_w + 1)

    ids = {}
    started = []

    def sem(name):
        return ids.setdefault(name, len(ids))

    def describe(name, src, dst, to):
        i = sem(name)
        return pltpu.make_async_remote_copy(src_ref=src, dst_ref=dst, send_sem=send_sem.at[i], recv_sem=recv_sem.at[i],
                                            device_id=to, device_id_type=MESH)

    def send(name, src, dst, to, when=None):
        copy = describe(name, src, dst, to)
        started.append((copy, when))
        if when is None:
            copy.start()
        else:
            pl.when(when)(copy.start)

    def arrive(name, dst, when=None):
        copy = describe(name, dst, dst, (sibling, x))
        if when is None:
            copy.wait_recv()
        else:
            pl.when(when)(copy.wait_recv)

    block = jnp.concatenate([filt[...].astype(F32), jnp.zeros((SLOT - OWN, PART), F32)], axis=0)
    f_out[...] = pltpu.roll(block, own_lead, 0).astype(BF16)
    f_in[...] = jnp.zeros_like(f_in)
    total_r[...] = jnp.zeros_like(total_r)

    barrier = pltpu.get_barrier_semaphore()
    cross = jnp.where(h == 0, before, after)
    peers = [(member(lax.rem(j + i, GROUP), z), x) for i in range(1, GROUP)]
    peers += [(at_place(y, z + 1, h), x), (at_place(y, z - 1, h), x), (cross, x)]
    peers += [(s, lax.rem(x + i, NX)) for i in range(1, NX)]
    mirror = at_place(x, z, 0)
    same_chip = x == y
    maybe = [(to_a, x, to_a != s), (to_b, x, own_two & (to_b != s)), (from_a, x, from_a != s), (from_b, x, my_two & (from_b != s)),
             (mirror + h, y, ~same_chip), (mirror + 1 - h, y, ~same_chip)]
    count = len(peers)
    for peer in peers:
        pl.semaphore_signal(barrier, inc=1, device_id=peer, device_id_type=MESH)
    for seq, section, when in maybe:
        count = count + when.astype(I32)

        @pl.when(when)
        def _(seq=seq, section=section):
            pl.semaphore_signal(barrier, inc=1, device_id=(seq, section), device_id_type=MESH)
    pl.semaphore_wait(barrier, count)

    send("pre_first", pre.at[pl.ds(0, EDGE)], halo_p.at[1], (before, x))
    send("pre_last", pre.at[pl.ds(ROWS - EDGE, EDGE)], halo_p.at[0], (after, x))
    send("emb_first", emb.at[pl.ds(0, EDGE)], halo_e.at[1], (before, x))
    send("emb_last", emb.at[pl.ds(ROWS // 2 - EDGE, EDGE)], halo_e.at[0], (after, x))
    send("filter_a", f_out, f_in.at[0], (to_a, x), to_a != s)
    send("filter_b", f_out, f_in.at[1], (to_b, x), own_two & (to_b != s))

    mine = pl.ds(pl.multiple_of(j * ROWS, ROWS), ROWS)
    row, lane = iota((QUARTER, 256), 0), iota((QUARTER, 256), 1)
    for i in range(GROUP):
        jj = lax.rem(j + i, GROUP)
        first = jj * CHUNK + x * QUARTER
        tile = jnp.minimum(first // 128, C_IN // 128 - 2)
        hit = (lane - row == first - tile * 128) & (row < CHUNK - x * QUARTER)
        seen = acts[:, pl.ds(pl.multiple_of(tile * 128, 128), 256)]
        piece = nt_dot(jnp.where(hit, 1.0, 0.0).astype(BF16), seen).astype(BF16)
        if i == 0:
            at[x, :, mine] = piece
        else:
            at_s[i - 1] = piece
            send(f"acts_{i}", at_s.at[i - 1], at.at[x, :, mine], (member(jj, z), x))

    for i, name in enumerate(("last", "first")):
        arrive("pre_" + name, halo_p.at[i])
        arrive("emb_" + name, halo_e.at[i])
    pick = (8 + iota((ROWS + 2 * EDGE, ROWS // 2 + 2 * EDGE), 0) // 2 == iota((ROWS + 2 * EDGE, ROWS // 2 + 2 * EDGE), 1)).astype(BF16)
    up = jnp.dot(pick, jnp.concatenate([halo_e[0], emb[...], halo_e[1]], axis=0), preferred_element_type=F32) * 0.5
    value = jnp.concatenate([halo_p[0], pre[...], halo_p[1]], axis=0).astype(F32)
    grad = up * gelu_slope(value)
    low = jnp.where(s > 0, 1.0, 0.0)
    high = jnp.where(s < SHARDS - 1, 1.0, 0.0)
    dzx[j, 0:EDGE] = jnp.concatenate([grad[8:16] * low, grad[ROWS + EDGE:ROWS + EDGE + 8] * high], axis=0).astype(BF16)
    dzx[j, EDGE:EDGE + ROWS] = grad[EDGE:EDGE + ROWS].astype(BF16)

    for i in (1, 3, 2):
        send(f"dz_{i}", dzx.at[j], dzx.at[j], (at_place(y + i, z, h), x))
    send("dz_sib_0", dzx.at[j], dzx.at[j], (sibling, x))

    def gather(t):
        if t == 0:
            arrive("filter_a", f_in.at[0], from_a != s)
            arrive("filter_b", f_in.at[1], my_two & (from_b != s))

            @pl.when(to_a == s)
            def _():
                f_in[0] = f_out[...]

            @pl.when(own_two & (to_b == s))
            def _():
                f_in[1] = f_out[...]

            f_slots[z] = jnp.where(iota((SLOT, PART), 0) < my_cut, f_in[0].astype(F32), f_in[1].astype(F32)).astype(BF16)
        for side, sign in ((0, 1), (1, -1)):
            if side == 1 and t == 4:
                continue
            slot = lax.rem(z - sign * t + NZ, NZ)
            if t > 0:
                arrive(f"gather_{side}_{t - 1}", f_slots.at[slot])
            if t < (4 if side == 0 else 3):
                send(f"gather_{side}_{t}", f_slots.at[slot], f_slots.at[slot], (at_place(y, z + sign, h), x))

    def shifts(b):
        edge = dzx[b, 0:EDGE].astype(F32)
        rim[8:16, :] = edge[0:8]
        rim[16:16 + ROWS, :] = dzx[b, EDGE:EDGE + ROWS].astype(F32)
        rim[16 + ROWS:24 + ROWS, :] = edge[8:16]
        place = pl.ds(pl.multiple_of(b * ROWS, ROWS), ROWS)
        for k in range(TAPS):
            dz[k, place, :] = rim[18 - k:18 - k + ROWS, :].astype(BF16)

    def from_y(i):
        b = 2 * lax.rem(y - i + NY, NY) + h
        arrive(f"dz_{i}", dzx.at[b])
        send(f"dz_sib_{i}", dzx.at[b], dzx.at[b], (sibling, x))
        shifts(b)

    def from_sibling(i):
        b = 2 * lax.rem(y - i + NY, NY) + 1 - h
        arrive(f"dz_sib_{i}", dzx.at[b])
        shifts(b)

    shifts(j)
    gather(0)
    for i in range(1, GROUP):
        b = lax.rem(j - i + GROUP, GROUP)
        arrive(f"acts_{i}", at.at[x, :, pl.ds(pl.multiple_of(b * ROWS, ROWS), ROWS)])
    for i in range(1, NX):
        send(f"acts_x_{i}", at.at[x], at.at[x], (s, lax.rem(x + i, NX)))
    from_sibling(0)
    gather(1)
    gather(2)
    from_y(1)
    from_y(3)
    gather(3)
    from_sibling(1)
    from_sibling(3)
    gather(4)
    from_y(2)
    from_sibling(2)
    for i in range(1, NX):
        arrive(f"acts_x_{i}", at.at[lax.rem(x - i + NX, NX)])

    part[SPACE:SPACE + 16, :] = jnp.zeros((16, PART), F32)
    columns = at[...].reshape(NX * QUARTER, GROUP * ROWS)
    for w in range(TAPS):
        rows = jnp.dot(columns, dz[tap_of(w)], preferred_element_type=F32)
        part[w * CHUNK:(w + 1) * CHUNK, :] = rows[0:CHUNK]

    HALF = SLOT // 2

    def reduce(t):
        for half in range(2):
            for side, sign in ((0, 1), (1, -1)):
                if t == 0 and side != half:
                    continue
                out, got = (s_r, g_r) if side == 0 else (s_l, g_l)
                dest = lax.rem(z + sign * (4 - t) + NZ, NZ)
                tile = (dest * OWN) // 16 * 16
                value = part[pl.ds(pl.multiple_of(tile + half * HALF, 16), HALF), :]
                if t > 0 and (t > 1 or side == half):
                    arrive(f"red_{side}_{t - 1}_{half}", got.at[t - 1, half])
                    value = value + got[t - 1, half].astype(F32)
                out[t, half] = value.astype(BF16)
                send(f"red_{side}_{t}_{half}", out.at[t, half], got.at[t, half], (at_place(y, z + sign, h), x))

    def reduce_end():
        for half in range(2):
            arrive(f"red_0_3_{half}", g_r.at[3, half])
            arrive(f"red_1_3_{half}", g_l.at[3, half])
            value = part[pl.ds(pl.multiple_of(my_tile + half * HALF, 16), HALF), :]
            value = value + g_r[3, half].astype(F32) + g_l[3, half].astype(F32)
            total_s[half * HALF:(half + 1) * HALF, :] = value.astype(BF16)
        send("total_a", total_s, total_r.at[0], (from_a, x), from_a != s)
        send("total_b", total_s, total_r.at[1], (from_b, x), my_two & (from_b != s))

    def pack():
        f_all[0:16, :] = jnp.zeros((16, PART), BF16)
        for u in range(NZ):
            base = u * OWN // 16 * 16
            f_all[base:base + 16, :] += f_slots[u, 0:16]
            f_all[base + 16:base + SLOT, :] = f_slots[u, 16:SLOT]

    def input_grad(i):
        dest = lax.rem(x + i, NX)
        for hh in range(2):
            place = pl.ds(pl.multiple_of((2 * dest + hh) * ROWS, ROWS), ROWS)
            total = jnp.zeros((CHUNK, ROWS), F32)
            for w in range(TAPS):
                total += nt_dot(f_all[w * CHUNK:(w + 1) * CHUNK, :], dz[tap_of(w), place, :])
            if i == 0:
                ig_own[:, hh * ROWS:(hh + 1) * ROWS] = total
            else:
                ig_s[i - 1, :, hh * ROWS:(hh + 1) * ROWS] = total.astype(BF16)
        if i > 0:
            send(f"ig_{i}", ig_s.at[i - 1], ig_r.at[i - 1], (s, dest))

    def input_grad_end():
        total = ig_own[...]
        for i in range(1, NX):
            arrive(f"ig_{i}", ig_r.at[i - 1])
            total += ig_r[i - 1].astype(F32)
        place = pl.ds(pl.multiple_of(h * CHUNK, 16), CHUNK)
        for hh in range(2):
            fin_s[hh] = total[:, hh * ROWS:(hh + 1) * ROWS].astype(BF16)
        other = 1 - h
        send("final_same", fin_s.at[h], ig_out.at[place], (mirror + h, y), ~same_chip)
        send("final_other", fin_s.at[other], ig_out.at[place], (jnp.where(same_chip, sibling, mirror + other), y))

        @pl.when(same_chip)
        def _():
            ig_out[place, :] = fin_s[h]

    reduce(0)
    pack()
    input_grad(1)
    reduce(1)
    input_grad(2)
    reduce(2)
    input_grad(3)
    reduce(3)
    input_grad(0)
    reduce_end()
    input_grad_end()

    arrive("total_a", total_r.at[0], to_a != s)
    arrive("total_b", total_r.at[1], own_two & (to_b != s))

    @pl.when(to_a == s)
    def _():
        total_r[0] = total_s[...]

    @pl.when(own_two & (to_b == s))
    def _():
        total_r[1] = total_s[...]

    rows = jnp.where(iota((SLOT, PART), 0) < own_cut, total_r[0].astype(F32), total_r[1].astype(F32))
    fg_out[...] = pltpu.roll(rows, lax.rem(SLOT - own_lead, SLOT), 0)[0:OWN] * scale

    arrive("final_same", ig_out.at[pl.ds(pl.multiple_of(h * CHUNK, 16), CHUNK)], ~same_chip)
    arrive("final_other", ig_out.at[pl.ds(pl.multiple_of((1 - h) * CHUNK, 16), CHUNK)])
    for copy, when in started:
        if when is None:
            copy.wait_send()
        else:
            pl.when(when)(copy.wait_send)


def shards(acts, pre_act, emb_grad, filters):
    total_rows = acts.shape[0] * lax.axis_size("seq")
    vmem = pl.BlockSpec(memory_space=pltpu.VMEM)
    across, filter_grad = pl.pallas_call(
        functools.partial(kernel, 1.0 / math.sqrt(total_rows)),
        out_shape=(jax.ShapeDtypeStruct((SLICE, ROWS), BF16), jax.ShapeDtypeStruct((OWN, PART), F32)),
        in_specs=[vmem] * 4,
        out_specs=(vmem, vmem),
        scratch_shapes=[
            pltpu.VMEM((SLOT, PART), BF16),
            pltpu.VMEM((2, SLOT, PART), BF16),
            pltpu.VMEM((NZ, SLOT, PART), BF16),
            pltpu.VMEM((SPACE + 16, PART), BF16),
            pltpu.VMEM((2, EDGE, PART), BF16),
            pltpu.VMEM((2, EDGE, PART), BF16),
            pltpu.VMEM((ROWS + 2 * EDGE, PART), F32),
            pltpu.VMEM((GROUP, ROWS + EDGE, PART), BF16),
            pltpu.VMEM((TAPS, GROUP * ROWS, PART), BF16),
            pltpu.VMEM((GROUP - 1, QUARTER, ROWS), BF16),
            pltpu.VMEM((NX, QUARTER, GROUP * ROWS), BF16),
            pltpu.VMEM((SPACE + 16, PART), F32),
            pltpu.VMEM((4, 2, SLOT // 2, PART), BF16),
            pltpu.VMEM((4, 2, SLOT // 2, PART), BF16),
            pltpu.VMEM((4, 2, SLOT // 2, PART), BF16),
            pltpu.VMEM((4, 2, SLOT // 2, PART), BF16),
            pltpu.VMEM((SLOT, PART), BF16),
            pltpu.VMEM((2, SLOT, PART), BF16),
            pltpu.VMEM((CHUNK, 2 * ROWS), F32),
            pltpu.VMEM((NX - 1, CHUNK, 2 * ROWS), BF16),
            pltpu.VMEM((NX - 1, CHUNK, 2 * ROWS), BF16),
            pltpu.VMEM((2, CHUNK, ROWS), BF16),
            pltpu.SemaphoreType.DMA((64,)),
            pltpu.SemaphoreType.DMA((64,)),
        ],
        compiler_params=pltpu.CompilerParams(collective_id=0, has_side_effects=True, vmem_limit_bytes=48 << 20),
    )(acts, pre_act, emb_grad, filters)
    return across.T, filter_grad


def solution(mesh):
    in_specs = (P("seq", None), P("seq", "section"), P("seq", "section"), P("seq", "section"))
    out_specs = (P("seq", "section"), P("seq", "section"))
    return jax.shard_map(shards, mesh=mesh, in_specs=in_specs, out_specs=out_specs, check_vma=False)
```

time: 343 us -> 69.9 us (0.20)
  waiting for transfers between devices: 276 us -> 0 us
  Pallas kernels: 0 us -> 62.8 us
  other arithmetic: 19.5 us -> 0 us
  local copies, waits for them, and re-layouts: 19.4 us -> 5.15 us
  between operations: 14.6 us -> 0.65 us
  matrix products: 7.19 us -> 0 us
  starting transfers between devices: 4.44 us -> 0 us
    unnamed x4 -> x0, waiting for transfers between devices: 179 us -> none
    all_gather x1 -> x0, waiting for transfers between devices: 70.9 us -> none  [shards(): piece = lax.all_gather(filters, 'seq', axis=0, tiled=True)]
    pallas_call x0 -> x1, Pallas kernels: none -> 62.8 us  [shards(): pl.pallas_call(functools.partial(kernel, 1.0 / math.sqrt(total_rows)), ou...]
    reduce_scatter x1 -> x0, waiting for transfers between devices: 25.3 us -> none  [shards(): lax.psum_scatter(partial_input, 'section', scatter_dimension=1, tiled=True)]
    add x1 -> x0, local copies, waits for them, and re-layouts: 8.73 us -> none  [shards(): total + jnp.where((tap_of == k)[None, :], product[4 - k:4 - k + rows], 0.0)]
    dot_general x6 -> x0, matrix products: 7.19 us -> none  [the longest x1 4.7 us: shards(): jnp.einsum('ro,no->rn', grad_rim, piece, preferred_element_type=jnp.float32)]
    add x1 -> x0, other arithmetic: 5.99 us -> none  [shards(): total + jnp.where((tap_of == k)[None, :], product[4 - k:4 - k + rows], 0.0)]
    mul x3 -> x0, other arithmetic: 5.66 us -> none  [the longest x1 4.65 us: shards(): jnp.concatenate([jnp.einsum('rc,ro->co', acts, grad_rim[4 - k:4 - k + row...]
  transfers between devices with their start and end apart: 5 -> 0, of which waited for: 4 -> 0; matrix products, arithmetic and copies ran while one was open for 13% -> 0% of each run, Pallas kernels for 0% -> 0%
where the time goes in v2:
time: 69.9 us; the launch traced here: 68.6 us
  Pallas kernels  62.8 us (90%)
  local copies, waits for them, and re-layouts  5.15 us (7%)
    pallas_call x1, Pallas kernels, shards(): pl.pallas_call(functools.partial(kernel, 1.0 / math.sqrt(total_rows)), ou...  62.8 us
    unnamed x10, local copies, waits for them, and re-layouts  5.15 us

profile of v2, /device:TPU:6, one launch (start us, length us, event | category | flops | bytes accessed | tf_op | source)
XLA Modules:
  0.0 68.6 jit_solution(14920274758823212776)
XLA Ops:
  0.6 0.0 copy-start
  0.6 1.1 %copy-done = bf16[256,1408]{1,0:T(8,128)(2,1)S(1)} copy-done((bf16[256,1408]{1,0:T(8,128)(2,1)S(1)}, bf16[256,1408]{1,0:T(8,128)(2,1)}, u32[]{:S(2)}) %copy-start) | copy-done | bytes 720920
  1.7 0.0 copy-start.1
  1.7 0.9 %copy-done.1 = bf16[256,384]{1,0:T(8,128)(2,1)S(1)} copy-done((bf16[256,384]{1,0:T(8,128)(2,1)S(1)}, bf16[256,384]{1,0:T(8,128)(2,1)}, u32[]{:S(2)}) %copy-start.1) | copy-done | bytes 196632
  2.7 0.0 copy-start.2
  2.7 0.9 %copy-done.2 = bf16[128,384]{1,0:T(8,128)(2,1)S(1)} copy-done((bf16[128,384]{1,0:T(8,128)(2,1)S(1)}, bf16[128,384]{1,0:T(8,128)(2,1)}, u32[]{:S(2)}) %copy-start.2) | copy-done | bytes 98328
  3.6 0.0 copy-start.3
  3.6 0.9 %copy-done.3 = bf16[110,384]{1,0:T(8,128)(2,1)S(1)} copy-done((bf16[110,384]{1,0:T(8,128)(2,1)S(1)}, bf16[110,384]{1,0:T(8,128)(2,1)}, u32[]{:S(2)}) %copy-start.3) | copy-done | bytes 84504
  4.5 62.8 %shard_map.59 = (bf16[352,256]{1,0:T(8,128)(2,1)S(1)}, f32[110,384]{1,0:T(8,128)S(1)}) custom-call(bf16[256,1408]{1,0:T(8,128)(2,1)S(1)} %copy-done, bf16[256,384]{1,0:T(8,128)(2,1)S(1)} %copy-done.1, bf16[128,384]{1,0:T(8,128)(2,1)S(1)} %copy-done.2, bf16[110,384]{1,0:T(8,128)(2,1)S(1)} %copy-done.3), custom_call_target="tpu_custom_call" | custom-call | tf_op jit(solution)/shard_map/pallas_call | solution.py:343
  67.2 0.7 copy.8
  67.9 0.7 copy.9
Async XLA Ops:
  0.6 1.1 %copy-start = (bf16[256,1408]{1,0:T(8,128)(2,1)S(1)}, bf16[256,1408]{1,0:T(8,128)(2,1)}, u32[]{:S(2)}) copy-start(bf16[256,1408]{1,0:T(8,128)(2,1)} %acts.1) | copy-start | bytes 2162692
  1.7 0.9 %copy-start.1 = (bf16[256,384]{1,0:T(8,128)(2,1)S(1)}, bf16[256,384]{1,0:T(8,128)(2,1)}, u32[]{:S(2)}) copy-start(bf16[256,384]{1,0:T(8,128)(2,1)} %pre.1) | copy-start | bytes 589828
  2.7 0.9 %copy-start.2 = (bf16[128,384]{1,0:T(8,128)(2,1)S(1)}, bf16[128,384]{1,0:T(8,128)(2,1)}, u32[]{:S(2)}) copy-start(bf16[128,384]{1,0:T(8,128)(2,1)} %emb.1) | copy-start | bytes 294916
  3.6 0.9 %copy-start.3 = (bf16[110,384]{1,0:T(8,128)(2,1)S(1)}, bf16[110,384]{1,0:T(8,128)(2,1)}, u32[]{:S(2)}) copy-start(bf16[110,384]{1,0:T(8,128)(2,1)} %filt.1) | copy-start | bytes 253444

commit v3 on v2

--- a/solution.py
+++ b/solution.py
@@ -41,8 +41,8 @@
     return lax.broadcasted_iota(I32, shape, axis)
 
 
-def kernel(scale, acts, pre, emb, filt, ig_out, fg_out, f_out, f_in, f_slots, f_all, halo_p, halo_e, rim, dzx, dz, at_s, at, part,
-           s_r, s_l, g_r, g_l, total_s, total_r, ig_own, ig_s, ig_r, fin_s, send_sem, recv_sem):
+def kernel(scale, acts_hbm, pre_hbm, emb_hbm, filt_hbm, ig_out, fg_out, acts, pre, emb, filt, f_out, f_in, f_slots, f_all, halo_p, halo_e, rim, dzx, dz, at_s, at, part,
+           s_r, s_l, g_r, g_l, total_s, total_r, ig_own, ig_s, ig_r, fin_s, load_sem, send_sem, recv_sem):
     s = lax.axis_index("seq")
     x = lax.axis_index("section")
     y, z, h = s // 16, lax.rem(s, 16) // 2, lax.rem(s, 2)
@@ -104,6 +104,12 @@
             copy.wait_recv()
         else:
             pl.when(when)(copy.wait_recv)
+
+    loads = []
+    for i, (src, dst) in enumerate(((filt_hbm, filt), (pre_hbm, pre), (emb_hbm, emb), (acts_hbm, acts))):
+        loads.append(pltpu.make_async_copy(src, dst, load_sem.at[i]))
+        loads[-1].start()
+    loads[0].wait()
 
     block = jnp.concatenate([filt[...].astype(F32), jnp.zeros((SLOT - OWN, PART), F32)], axis=0)
     f_out[...] = pltpu.roll(block, own_lead, 0).astype(BF16)
@@ -128,6 +134,8 @@
         @pl.when(when)
         def _(seq=seq, section=section):
             pl.semaphore_signal(barrier, inc=1, device_id=(seq, section), device_id_type=MESH)
+    for load in loads[1:]:
+        load.wait()
     pl.semaphore_wait(barrier, count)
 
     send("pre_first", pre.at[pl.ds(0, EDGE)], halo_p.at[1], (before, x))
@@ -212,21 +220,19 @@
         shifts(b)
 
     shifts(j)
-    gather(0)
     for i in range(1, GROUP):
         b = lax.rem(j - i + GROUP, GROUP)
         arrive(f"acts_{i}", at.at[x, :, pl.ds(pl.multiple_of(b * ROWS, ROWS), ROWS)])
     for i in range(1, NX):
         send(f"acts_x_{i}", at.at[x], at.at[x], (s, lax.rem(x + i, NX)))
     from_sibling(0)
-    gather(1)
-    gather(2)
+    gather(0)
     from_y(1)
     from_y(3)
-    gather(3)
+    gather(1)
     from_sibling(1)
     from_sibling(3)
-    gather(4)
+    gather(2)
     from_y(2)
     from_sibling(2)
     for i in range(1, NX):
@@ -272,47 +278,57 @@
             f_all[base:base + 16, :] += f_slots[u, 0:16]
             f_all[base + 16:base + SLOT, :] = f_slots[u, 16:SLOT]
 
-    def input_grad(i):
+    def input_grad(i, hh):
         dest = lax.rem(x + i, NX)
-        for hh in range(2):
-            place = pl.ds(pl.multiple_of((2 * dest + hh) * ROWS, ROWS), ROWS)
-            total = jnp.zeros((CHUNK, ROWS), F32)
-            for w in range(TAPS):
-                total += nt_dot(f_all[w * CHUNK:(w + 1) * CHUNK, :], dz[tap_of(w), place, :])
-            if i == 0:
-                ig_own[:, hh * ROWS:(hh + 1) * ROWS] = total
-            else:
-                ig_s[i - 1, :, hh * ROWS:(hh + 1) * ROWS] = total.astype(BF16)
-        if i > 0:
-            send(f"ig_{i}", ig_s.at[i - 1], ig_r.at[i - 1], (s, dest))
-
-    def input_grad_end():
-        total = ig_own[...]
+        place = pl.ds(pl.multiple_of((2 * dest + hh) * ROWS, ROWS), ROWS)
+        total = jnp.zeros((CHUNK, ROWS), F32)
+        for w in range(TAPS):
+            total += nt_dot(f_all[w * CHUNK:(w + 1) * CHUNK, :], dz[tap_of(w), place, :])
+        if i == 0:
+            ig_own[hh] = total
+        else:
+            ig_s[i - 1, hh] = total.astype(BF16)
+            send(f"ig_{i}_{hh}", ig_s.at[i - 1, hh], ig_r.at[i - 1, hh], (s, dest))
+
+    own_rows = pl.ds(pl.multiple_of(h * CHUNK, 16), CHUNK)
+    other_rows = pl.ds(pl.multiple_of((1 - h) * CHUNK, 16), CHUNK)
+    final_base = [sem("final_0"), sem("final_1")][0]
+
+    def input_grad_end(hh):
+        total = ig_own[hh]
         for i in range(1, NX):
-            arrive(f"ig_{i}", ig_r.at[i - 1])
-            total += ig_r[i - 1].astype(F32)
-        place = pl.ds(pl.multiple_of(h * CHUNK, 16), CHUNK)
-        for hh in range(2):
-            fin_s[hh] = total[:, hh * ROWS:(hh + 1) * ROWS].astype(BF16)
-        other = 1 - h
-        send("final_same", fin_s.at[h], ig_out.at[place], (mirror + h, y), ~same_chip)
-        send("final_other", fin_s.at[other], ig_out.at[place], (jnp.where(same_chip, sibling, mirror + other), y))
-
-        @pl.when(same_chip)
+            arrive(f"ig_{i}_{hh}", ig_r.at[i - 1, hh])
+            total += ig_r[i - 1, hh].astype(F32)
+        fin_s[hh] = total.astype(BF16)
+        here = same_chip & (h == hh)
+        copy = pltpu.make_async_remote_copy(src_ref=fin_s.at[hh], dst_ref=ig_out.at[own_rows], send_sem=send_sem.at[final_base + hh],
+                                            recv_sem=recv_sem.at[final_base + lax.rem(h + hh, 2)], device_id=(mirror + hh, y),
+                                            device_id_type=MESH)
+        pl.when(~here)(copy.start)
+        started.append((copy, ~here))
+
+        @pl.when(here)
         def _():
-            ig_out[place, :] = fin_s[h]
-
+            ig_out[own_rows, :] = fin_s[hh]
+
+    gather(3)
     reduce(0)
+    gather(4)
     pack()
-    input_grad(1)
+    input_grad(1, 0)
     reduce(1)
-    input_grad(2)
+    input_grad(2, 0)
+    input_grad(3, 0)
     reduce(2)
-    input_grad(3)
+    input_grad(0, 0)
+    input_grad(1, 1)
+    input_grad(2, 1)
     reduce(3)
-    input_grad(0)
+    input_grad(3, 1)
+    input_grad(0, 1)
+    input_grad_end(0)
     reduce_end()
-    input_grad_end()
+    input_grad_end(1)
 
     arrive("total_a", total_r.at[0], to_a != s)
     arrive("total_b", total_r.at[1], own_two & (to_b != s))
@@ -328,8 +344,8 @@
     rows = jnp.where(iota((SLOT, PART), 0) < own_cut, total_r[0].astype(F32), total_r[1].astype(F32))
     fg_out[...] = pltpu.roll(rows, lax.rem(SLOT - own_lead, SLOT), 0)[0:OWN] * scale
 
-    arrive("final_same", ig_out.at[pl.ds(pl.multiple_of(h * CHUNK, 16), CHUNK)], ~same_chip)
-    arrive("final_other", ig_out.at[pl.ds(pl.multiple_of((1 - h) * CHUNK, 16), CHUNK)])
+    arrive("final_0", ig_out.at[own_rows], ~same_chip)
+    arrive("final_1", ig_out.at[other_rows])
     for copy, when in started:
         if when is None:
             copy.wait_send()
@@ -343,9 +359,13 @@
     across, filter_grad = pl.pallas_call(
         functools.partial(kernel, 1.0 / math.sqrt(total_rows)),
         out_shape=(jax.ShapeDtypeStruct((SLICE, ROWS), BF16), jax.ShapeDtypeStruct((OWN, PART), F32)),
-        in_specs=[vmem] * 4,
+        in_specs=[pl.BlockSpec(memory_space=pl.ANY)] * 4,
         out_specs=(vmem, vmem),
         scratch_shapes=[
+            pltpu.VMEM((ROWS, C_IN), BF16),
+            pltpu.VMEM((ROWS, PART), BF16),
+            pltpu.VMEM((ROWS // 2, PART), BF16),
+            pltpu.VMEM((OWN, PART), BF16),
             pltpu.VMEM((SLOT, PART), BF16),
             pltpu.VMEM((2, SLOT, PART), BF16),
             pltpu.VMEM((NZ, SLOT, PART), BF16),
@@ -364,14 +384,15 @@
             pltpu.VMEM((4, 2, SLOT // 2, PART), BF16),
             pltpu.VMEM((SLOT, PART), BF16),
             pltpu.VMEM((2, SLOT, PART), BF16),
-            pltpu.VMEM((CHUNK, 2 * ROWS), F32),
-            pltpu.VMEM((NX - 1, CHUNK, 2 * ROWS), BF16),
-            pltpu.VMEM((NX - 1, CHUNK, 2 * ROWS), BF16),
+            pltpu.VMEM((2, CHUNK, ROWS), F32),
+            pltpu.VMEM((NX - 1, 2, CHUNK, ROWS), BF16),
+            pltpu.VMEM((NX - 1, 2, CHUNK, ROWS), BF16),
             pltpu.VMEM((2, CHUNK, ROWS), BF16),
+            pltpu.SemaphoreType.DMA((4,)),
             pltpu.SemaphoreType.DMA((64,)),
             pltpu.SemaphoreType.DMA((64,)),
         ],
-        compiler_params=pltpu.CompilerParams(collective_id=0, has_side_effects=True, vmem_limit_bytes=48 << 20),
+        compiler_params=pltpu.CompilerParams(collective_id=0, has_side_effects=True, vmem_limit_bytes=58 << 20),
     )(acts, pre_act, emb_grad, filters)
     return across.T, filter_grad
 

time: 69.9 us -> 63.6 us (0.910)
  Pallas kernels: 62.8 us -> 59.5 us
  local copies, waits for them, and re-layouts: 5.15 us -> 2.32 us
    pallas_call x1, Pallas kernels: 62.8 us -> 59.5 us  [shards(): pl.pallas_call(functools.partial(kernel, 1.0 / math.sqrt(total_rows)), ou...]
    unnamed x10 -> x4, local copies, waits for them, and re-layouts: 5.15 us -> 2.32 us
where the time goes in v3:
time: 63.6 us; the launch traced here: 62.5 us
  Pallas kernels  59.5 us (94%)
  local copies, waits for them, and re-layouts  2.32 us (4%)
  between operations  0.65 us (1%)
    pallas_call x1, Pallas kernels, shards(): pl.pallas_call(functools.partial(kernel, 1.0 / math.sqrt(total_rows)), ou...  59.5 us
    unnamed x4, local copies, waits for them, and re-layouts  2.32 us

profile of v3, /device:TPU:6, one launch (start us, length us, event | category | flops | bytes accessed | tf_op | source)
XLA Modules:
  0.0 62.5 jit_solution(6250426690557480417)
XLA Ops:
  0.6 59.5 %shard_map.59 = (bf16[352,256]{1,0:T(8,128)(2,1)}, f32[110,384]{1,0:T(8,128)}) custom-call(bf16[256,1408]{1,0:T(8,128)(2,1)} %acts_hbm.1, bf16[256,384]{1,0:T(8,128)(2,1)} %pre_hbm.1, bf16[128,384]{1,0:T(8,128)(2,1)} %emb_hbm.1, bf16[110,384]{1,0:T(8,128)(2,1)} %filt_hbm.1), custom_call_target="tpu_custom_call" | custom-call | tf_op jit(solution)/shard_map/pallas_call | solution.py:359
  60.2 0.0 copy-start
  60.2 1.6 %copy.8 = bf16[256,352]{0,1:T(8,128)(2,1)} copy(bf16[256,352]{0,1:T(8,128)(2,1)} %bitcast.1) | data formatting | bytes 360448
  61.8 0.0 copy-done
  61.8 0.7 %copy.9 = f32[110,384]{1,0:T(8,128)} copy(f32[110,384]{1,0:T(8,128)S(1)} %copy-done) | data formatting | bytes 337920
Async XLA Ops:
  60.2 1.7 %copy-start = (f32[110,384]{1,0:T(8,128)S(1)}, f32[110,384]{1,0:T(8,128)}, u32[]{:S(2)}) copy-start(f32[110,384]{1,0:T(8,128)} %get-tuple-element.9) | copy-start | bytes 506884

commit v4 on v3

--- a/solution.py
+++ b/solution.py
@@ -220,16 +220,16 @@
         shifts(b)
 
     shifts(j)
+    from_sibling(0)
+    gather(0)
     for i in range(1, GROUP):
         b = lax.rem(j - i + GROUP, GROUP)
         arrive(f"acts_{i}", at.at[x, :, pl.ds(pl.multiple_of(b * ROWS, ROWS), ROWS)])
     for i in range(1, NX):
         send(f"acts_x_{i}", at.at[x], at.at[x], (s, lax.rem(x + i, NX)))
-    from_sibling(0)
-    gather(0)
+    gather(1)
     from_y(1)
     from_y(3)
-    gather(1)
     from_sibling(1)
     from_sibling(3)
     gather(2)
@@ -311,8 +311,8 @@
         def _():
             ig_out[own_rows, :] = fin_s[hh]
 
+    reduce(0)
     gather(3)
-    reduce(0)
     gather(4)
     pack()
     input_grad(1, 0)

time: 63.6 us -> 63.2 us (level)
  no operation moved by 1% of the time
where the time goes in v4:
time: 63.2 us; the launch traced here: 62.2 us
  Pallas kernels  59.2 us (94%)
  local copies, waits for them, and re-layouts  2.32 us (4%)
  between operations  0.65 us (1%)
    pallas_call x1, Pallas kernels, shards(): pl.pallas_call(functools.partial(kernel, 1.0 / math.sqrt(total_rows)), ou...  59.2 us
    unnamed x4, local copies, waits for them, and re-layouts  2.32 us

profile of v4, /device:TPU:6, one launch (start us, length us, event | category | flops | bytes accessed | tf_op | source)
XLA Modules:
  0.0 62.2 jit_solution(7730163845583242535)
XLA Ops:
  0.6 59.2 %shard_map.59 = (bf16[352,256]{1,0:T(8,128)(2,1)}, f32[110,384]{1,0:T(8,128)}) custom-call(bf16[256,1408]{1,0:T(8,128)(2,1)} %acts_hbm.1, bf16[256,384]{1,0:T(8,128)(2,1)} %pre_hbm.1, bf16[128,384]{1,0:T(8,128)(2,1)} %emb_hbm.1, bf16[110,384]{1,0:T(8,128)(2,1)} %filt_hbm.1), custom_call_target="tpu_custom_call" | custom-call | tf_op jit(solution)/shard_map/pallas_call | solution.py:359
  59.8 0.0 copy-start
  59.8 1.6 %copy.8 = bf16[256,352]{0,1:T(8,128)(2,1)} copy(bf16[256,352]{0,1:T(8,128)(2,1)} %bitcast.1) | data formatting | bytes 360448
  61.5 0.0 copy-done
  61.5 0.7 %copy.9 = f32[110,384]{1,0:T(8,128)} copy(f32[110,384]{1,0:T(8,128)S(1)} %copy-done) | data formatting | bytes 337920
Async XLA Ops:
  59.8 1.7 %copy-start = (f32[110,384]{1,0:T(8,128)S(1)}, f32[110,384]{1,0:T(8,128)}, u32[]{:S(2)}) copy-start(f32[110,384]{1,0:T(8,128)} %get-tuple-element.9) | copy-start | bytes 506884
